TPU v7x, 256 devices: a whole 4x4x8 slice. The times are simulated.
256 devices in a mesh: pulse: 8 (over y, core), tile: 32 (over x, z).
Axes of the slice: x: 4, y: 4, z: 8, core: 2. Of those that a mesh axis runs over, the one named last changes fastest.
Arguments:
- echoes: bfloat16 [512, 2, 2, 16384], P(('pulse', 'tile')), may hold values from -6 to 6
- pulse_slope: bfloat16 [512, 2], P(('pulse', 'tile')), may hold values from -0.023925781 to 0.023925781
- pulse_shift: bfloat16 [512, 2], P(('pulse', 'tile')), may hold values from -3.140625 to 3.140625
- footprint: int32 [8, 32, 32], P('pulse'), may hold values from -1 to 63, as said below
- band_start: int32 [1024], P('tile'), may hold values from 0 to 13216
- row_phase: float32 [1024], P('tile'), may hold values from -1 to 1
Outputs:
- formed_image: float32 [2, 1024, 4096], P(None, 'tile', 'pulse')
Inputs may be any that keep to these rules, and one draw needn't show every extreme that they name: footprint[g, t] lists in rising order the numbers of group g's blocks whose echoes reach row strip t, then -1 to the end. It names at most one block of each run of 2 numbers that starts at a multiple of 2. In every group some list has 32 entries.
All inputs are finite; a program needn't handle non-finite values.
Results may differ from a plain program's by a relative error of at most 0.0039.
Values may be sent and summed in bfloat16 or wider, within the bound.
No kernel may reach another device: no remote copies, remote signals or barrier semaphores. Data moves between devices by JAX's collectives and lax.ppermute only.
A program may use at most 64 MiB of HBM per device.

v0:
```python
import jax
import jax.numpy as jnp
from jax import lax
from jax.sharding import PartitionSpec as P

NCOL = 4096
PB = 2
ITERS = 2
step_size = 0.5
tv_weight = 0.4
floor_square = 0.25


def padded_2(value, sides, width):
    for axis, dim in sides:
        size, length = (lax.axis_size(axis), value.shape[dim])
        up = [(i, (i + 1) % size) for i in range(size - 1)]
        down = [(j, i) for i, j in up]
        last = lax.slice_in_dim(value, length - width, length, axis=dim)
        leading = lax.slice_in_dim(value, 0, width, axis=dim)
        before = lax.ppermute(last, axis, up)
        after = lax.ppermute(leading, axis, down)
        value = jnp.concatenate([before, value, after], axis=dim)
    return value


def cubic_table():
    columns = jnp.arange(128, dtype=jnp.int32)
    quarter_pos = 3 * columns + 4
    base_tap = quarter_pos // 4
    fraction = (quarter_pos % 4).astype(jnp.float32) / 4.0
    fraction_sq = fraction * fraction
    fraction_cube = fraction_sq * fraction
    weights = [
        (-fraction_cube + 2.0 * fraction_sq - fraction) * 0.5,
        (3.0 * fraction_cube - 5.0 * fraction_sq + 2.0) * 0.5,
        (-3.0 * fraction_cube + 4.0 * fraction_sq + fraction) * 0.5,
        (fraction_cube - fraction_sq) * 0.5,
    ]
    tap_rows = jnp.arange(128, dtype=jnp.int32)[:, None]
    cubic_weights = jnp.zeros((128, 128), jnp.float32)
    for tap_shift, weight in zip(range(-1, 3), weights):
        cubic_weights = cubic_weights + jnp.where(
            tap_rows == (base_tap + tap_shift)[None, :], weight[None, :], 0.0
        )
    return cubic_weights


def block_image(block_echo, block_slope, block_shift, band_start, row_phase, cubic_weights):
    pulses = block_echo.shape[0]
    row_count = band_start.shape[0]
    col_blocks = NCOL // 128
    window_span = 96 * (col_blocks + 1)
    flat_echo = block_echo.reshape(pulses * 2, block_echo.shape[2])
    segments = jax.vmap(
        lambda row_start: lax.dynamic_slice_in_dim(flat_echo, row_start, window_span, axis=1)
    )(band_start)
    leading = segments[..., : 96 * col_blocks].reshape(row_count, pulses * 2, col_blocks, 96)
    trailing = segments[..., 96:].reshape(row_count, pulses * 2, col_blocks, 96)[..., :32]
    windows = jnp.concatenate([leading, trailing], axis=-1)
    windows = (
        jnp.transpose(windows, (0, 2, 1, 3))
        .reshape(row_count, col_blocks, pulses, 2, 128)
        .astype(jnp.float32)
    )
    slopes = block_slope.astype(jnp.float32)
    shifts = block_shift.astype(jnp.float32)
    block_pos = (128 * jnp.arange(col_blocks, dtype=jnp.int32)).astype(jnp.float32)
    angle_grid = (
        shifts[None, None, :] * row_phase[:, None, None]
        + slopes[None, None, :] * block_pos[None, :, None]
    )
    cosine = jnp.cos(angle_grid)[..., None]
    sines = jnp.sin(angle_grid)[..., None]
    real_part = windows[:, :, :, 0]
    imag_part = windows[:, :, :, 1]
    turned_re = real_part * cosine - imag_part * sines
    turned_im = real_part * sines + imag_part * cosine
    turned = (
        jnp.stack([turned_re, turned_im], axis=3)
        .astype(jnp.bfloat16)
        .reshape(row_count * col_blocks, pulses * 256)
    )
    column_pos = jnp.arange(128, dtype=jnp.int32).astype(jnp.float32)
    column_ramp = slopes[:, None] * column_pos[None, :]
    kernel_re = cubic_weights[None] * jnp.cos(column_ramp)[:, None, :]
    kernel_im = cubic_weights[None] * jnp.sin(column_ramp)[:, None, :]
    upper_rows = jnp.concatenate([kernel_re, kernel_im], axis=2)
    bottom = jnp.concatenate([-kernel_im, kernel_re], axis=2)
    kernel = jnp.stack([upper_rows, bottom], axis=1).astype(jnp.bfloat16).reshape(pulses * 256, 256)
    product = jnp.dot(turned, kernel, preferred_element_type=jnp.float32)
    return product.reshape(row_count, col_blocks, 256)


def add_used(
    running, echo_all, slope_all, shift_all, slots, used_count, band_start, row_phase, cubic_weights
):
    slot_count = slots.shape[0]

    def add_pair(pair_index, partial_sum):
        first_slot = slots[2 * pair_index]
        second_slot = slots[jnp.minimum(2 * pair_index + 1, slot_count - 1)]
        second_used = 2 * pair_index + 1 < used_count
        second_echo = jnp.where(second_used, echo_all[second_slot], jnp.zeros_like(echo_all[0]))
        echo_pair = jnp.concatenate([echo_all[first_slot], second_echo], axis=0)
        slope_pair = jnp.concatenate([slope_all[first_slot], slope_all[second_slot]], axis=0)
        shift_pair = jnp.concatenate([shift_all[first_slot], shift_all[second_slot]], axis=0)
        return partial_sum + block_image(
            echo_pair, slope_pair, shift_pair, band_start, row_phase, cubic_weights
        )

    return lax.fori_loop(0, (used_count + 1) // 2, add_pair, running)


def tv_update(field, padded, base_image, row_anchor, col_anchor, grid_rows, grid_cols):
    row_count = field.shape[1]
    col_count = field.shape[2]
    grad_rows = (
        padded[:, 1 : row_count + 2, 0 : col_count + 1]
        - padded[:, 0 : row_count + 1, 0 : col_count + 1]
    )
    grad_cols = (
        padded[:, 0 : row_count + 1, 1 : col_count + 2]
        - padded[:, 0 : row_count + 1, 0 : col_count + 1]
    )
    row_ids = row_anchor - 1 + jnp.arange(row_count + 1, dtype=jnp.int32)
    col_ids = col_anchor - 1 + jnp.arange(col_count + 1, dtype=jnp.int32)
    inside = (row_ids >= 0)[:, None] & (col_ids >= 0)[None, :]
    grad_rows = jnp.where((inside & (row_ids < grid_rows - 1)[:, None])[None], grad_rows, 0.0)
    grad_cols = jnp.where((inside & (col_ids < grid_cols - 1)[None, :])[None], grad_cols, 0.0)
    magnitude = jnp.sqrt(
        jnp.sum(grad_rows * grad_rows + grad_cols * grad_cols, axis=0) + floor_square
    )
    flux_rows = grad_rows / magnitude[None]
    flux_cols = grad_cols / magnitude[None]
    divergence = (
        flux_rows[:, 1:, 1:] - flux_rows[:, :-1, 1:] + flux_cols[:, 1:, 1:] - flux_cols[:, 1:, :-1]
    )
    return field - step_size * (field - base_image - tv_weight * divergence)


def to_image(blocks):
    row_count = blocks.shape[0]
    col_count = blocks.shape[1] * 128
    real_plane = blocks[..., :128].reshape(row_count, col_count)
    imag_plane = blocks[..., 128:].reshape(row_count, col_count)
    return jnp.stack([real_plane, imag_plane])


def body(echoes, pulse_slope, pulse_shift, footprint, band_start, row_phase):
    tile_count = lax.axis_size("tile")
    groups = lax.axis_size("pulse")
    tile_index = lax.axis_index("tile")
    group_index = lax.axis_index("pulse")
    row_count = band_start.shape[0]
    col_blocks = NCOL // 128
    cubic_weights = cubic_table()
    footprints = footprint[0]
    own_list = lax.dynamic_index_in_dim(footprints, tile_index, axis=0, keepdims=False)
    zero_image = jnp.zeros((row_count, col_blocks, 256), jnp.float32)
    piece_echo = lax.all_gather(echoes, "tile", axis=0, tiled=True)
    piece_slope = lax.all_gather(pulse_slope, "tile", axis=0, tiled=True)
    piece_shift = lax.all_gather(pulse_shift, "tile", axis=0, tiled=True)
    piece_count = piece_echo.shape[0]
    positions = jnp.arange(piece_count, dtype=jnp.int32)
    is_used = jnp.any(positions[:, None] == own_list[None, :], axis=1)
    ordering = jnp.argsort(jnp.where(is_used, 0, piece_count) + positions)
    used_total = jnp.sum(is_used.astype(jnp.int32))
    partial_image = add_used(
        zero_image,
        piece_echo,
        piece_slope,
        piece_shift,
        ordering,
        used_total,
        band_start,
        row_phase,
        cubic_weights,
    )
    normalize = float(PB * tile_count * groups) ** (-0.5)
    grid_rows = tile_count * row_count
    row_anchor = tile_index * row_count
    whole = lax.psum(partial_image, "pulse")
    base_image = to_image(whole) * normalize
    field = base_image
    for iteration in range(ITERS):
        padded = padded_2(field, (("tile", 1),), 1)
        padded = jnp.pad(padded, ((0, 0), (0, 0), (1, 1)))
        field = tv_update(field, padded, base_image, row_anchor, 0, grid_rows, NCOL)
    share_width = NCOL // groups
    return lax.dynamic_slice_in_dim(field, group_index * share_width, share_width, axis=2)


def solution(mesh):
    in_specs = (
        P(("pulse", "tile"), None, None, None),
        P(("pulse", "tile"), None),
        P(("pulse", "tile"), None),
        P("pulse", None, None),
        P("tile"),
        P("tile"),
    )
    out_specs = P(None, "tile", "pulse")
    return jax.shard_map(body, mesh=mesh, in_specs=in_specs, out_specs=out_specs, check_vma=False)
```

profile of v0, /device:TPU:64, one launch (start us, length us, event | category | flops | bytes accessed | tf_op | source)
XLA Modules:
  0.0 1211.1 jit_solution(6912679305393457067)
XLA Ops:
  8.7 2.0 sort.17
  10.7 40.3 %all-gather = bf16[32,2,2]{2,1,0:T(2,128)(2,1)S(1)} all-gather(bf16[1,2,2]{2,1,0:T(2,128)(2,1)} %bitcast.74), channel_id=1, replica_groups=mesh['pulse'=8,'tile'=32] {'tile'}, dimensions={0}, use_global_device_ids=true | all-gather | bytes 264 | tf_op jit(solution)/shard_map/all_gather | solution.py:163
  51.0 37.3 %all-gather.1 = bf16[32,2,2]{2,1,0:T(2,128)(2,1)S(1)} all-gather(bf16[1,2,2]{2,1,0:T(2,128)(2,1)} %bitcast.75), channel_id=1, replica_groups=mesh['pulse'=8,'tile'=32] {'tile'}, dimensions={0}, use_global_device_ids=true | all-gather | bytes 264 | tf_op jit(solution)/shard_map/all_gather | solution.py:162
  88.4 20.5 %all-gather.4.cloned.1.call-done = bf16[64,2,2,16384]{3,2,1,0:T(2,128)(2,1)} async-done(((bf16[2,2,2,16384]{3,2,1,0:T(2,128)(2,1)}), bf16[64,2,2,16384]{3,2,1,0:T(2,128)(2,1)}) %all-gather.4.cloned.1.call-update) | async-done | bytes 8388624 | tf_op jit(solution)/shard_map/all_gather | solution.py:161
  109.1 437.2 %while.17 = (s32[]{:T(128)}, f32[32,32,256]{2,1,0:T(8,128)S(1)}, s32[]{:T(128)}, s32[64]{0:T(128)S(1)}, bf16[64,2,2,16384]{3,2,1,0:T(2,128)(2,1)}, /*index=5*/s3...) while((s32[]{:T(128)}, f32[32,32,256]{2,1,0:T(8,128)S(1)}, ...), condition=%wide.region_4.5_spmd.clone.clone, body=%wide.region_3.4_spmd.clone.clone.sunk | while | flops 548656192 | bytes 41472712 | solution.py:112
  113.8 1.2 dynamic-slice_bitcast_fusion.2
  115.5 39.0 %while.18 = (s32[]{:T(128)}, bf16[8,16384]{1,0:T(8,128)(2,1)S(1)}, s32[32,2]{0,1:T(2,128)S(1)}, bf16[32,8,3168]{2,1,0:T(8,128)(2,1)S(1)}, s32[]{:T(128)}) while((s32[]{:T(128)}, bf16[8,16384]{1,0:T(8,128)(2,1)S(1)}, s32[32,2]{0,1:T(2,128)S(1)}, bf16[32,8,3168]{2,1,0:T(8,128)(2,1)S(1)}, s32[]{:T(128)}) %tuple.94), condition=%wide.while_cond, body=%wide.while_body.sunk | while | flops 2 | bytes 102497 | solution.py:56
  154.5 2.4 fusion.59
  157.0 3.6 reshape.426
  160.6 4.5 reshape.427
  165.1 2.6 maximum_convert_fusion.6
  169.0 1.4 subtract_convert_fusion.2
  176.3 1.2 dynamic-slice_bitcast_fusion.2
  178.0 39.0 %while.18 = (s32[]{:T(128)}, bf16[8,16384]{1,0:T(8,128)(2,1)S(1)}, s32[32,2]{0,1:T(2,128)S(1)}, bf16[32,8,3168]{2,1,0:T(8,128)(2,1)S(1)}, s32[]{:T(128)}) while((s32[]{:T(128)}, bf16[8,16384]{1,0:T(8,128)(2,1)S(1)}, s32[32,2]{0,1:T(2,128)S(1)}, bf16[32,8,3168]{2,1,0:T(8,128)(2,1)S(1)}, s32[]{:T(128)}) %tuple.94), condition=%wide.while_cond, body=%wide.while_body.sunk | while | flops 2 | bytes 102497 | solution.py:56
  217.0 2.4 fusion.59
  219.4 3.6 reshape.426
  223.0 4.5 reshape.427
  227.6 2.6 maximum_convert_fusion.6
  231.5 1.4 subtract_convert_fusion.2
  238.7 1.2 dynamic-slice_bitcast_fusion.2
  240.4 39.0 %while.18 = (s32[]{:T(128)}, bf16[8,16384]{1,0:T(8,128)(2,1)S(1)}, s32[32,2]{0,1:T(2,128)S(1)}, bf16[32,8,3168]{2,1,0:T(8,128)(2,1)S(1)}, s32[]{:T(128)}) while((s32[]{:T(128)}, bf16[8,16384]{1,0:T(8,128)(2,1)S(1)}, s32[32,2]{0,1:T(2,128)S(1)}, bf16[32,8,3168]{2,1,0:T(8,128)(2,1)S(1)}, s32[]{:T(128)}) %tuple.94), condition=%wide.while_cond, body=%wide.while_body.sunk | while | flops 2 | bytes 102497 | solution.py:56
  279.4 2.4 fusion.59
  281.9 3.6 reshape.426
  285.5 4.5 reshape.427
  290.0 2.6 maximum_convert_fusion.6
  294.0 1.4 subtract_convert_fusion.2
  301.2 1.2 dynamic-slice_bitcast_fusion.2
  302.9 39.0 %while.18 = (s32[]{:T(128)}, bf16[8,16384]{1,0:T(8,128)(2,1)S(1)}, s32[32,2]{0,1:T(2,128)S(1)}, bf16[32,8,3168]{2,1,0:T(8,128)(2,1)S(1)}, s32[]{:T(128)}) while((s32[]{:T(128)}, bf16[8,16384]{1,0:T(8,128)(2,1)S(1)}, s32[32,2]{0,1:T(2,128)S(1)}, bf16[32,8,3168]{2,1,0:T(8,128)(2,1)S(1)}, s32[]{:T(128)}) %tuple.94), condition=%wide.while_cond, body=%wide.while_body.sunk | while | flops 2 | bytes 102497 | solution.py:56
  341.9 2.4 fusion.59
  344.3 3.6 reshape.426
  347.9 4.5 reshape.427
  352.5 2.6 maximum_convert_fusion.6
  356.4 1.4 subtract_convert_fusion.2
  363.6 1.2 dynamic-slice_bitcast_fusion.2
  365.3 39.0 %while.18 = (s32[]{:T(128)}, bf16[8,16384]{1,0:T(8,128)(2,1)S(1)}, s32[32,2]{0,1:T(2,128)S(1)}, bf16[32,8,3168]{2,1,0:T(8,128)(2,1)S(1)}, s32[]{:T(128)}) while((s32[]{:T(128)}, bf16[8,16384]{1,0:T(8,128)(2,1)S(1)}, s32[32,2]{0,1:T(2,128)S(1)}, bf16[32,8,3168]{2,1,0:T(8,128)(2,1)S(1)}, s32[]{:T(128)}) %tuple.94), condition=%wide.while_cond, body=%wide.while_body.sunk | while | flops 2 | bytes 102497 | solution.py:56
  404.4 2.4 fusion.59
  406.8 3.6 reshape.426
  410.4 4.5 reshape.427
  414.9 2.6 maximum_convert_fusion.6
  418.9 1.4 subtract_convert_fusion.2
  426.1 1.2 dynamic-slice_bitcast_fusion.2
  427.8 39.0 %while.18 = (s32[]{:T(128)}, bf16[8,16384]{1,0:T(8,128)(2,1)S(1)}, s32[32,2]{0,1:T(2,128)S(1)}, bf16[32,8,3168]{2,1,0:T(8,128)(2,1)S(1)}, s32[]{:T(128)}) while((s32[]{:T(128)}, bf16[8,16384]{1,0:T(8,128)(2,1)S(1)}, s32[32,2]{0,1:T(2,128)S(1)}, bf16[32,8,3168]{2,1,0:T(8,128)(2,1)S(1)}, s32[]{:T(128)}) %tuple.94), condition=%wide.while_cond, body=%wide.while_body.sunk | while | flops 2 | bytes 102497 | solution.py:56
  466.8 2.4 fusion.59
  469.2 3.6 reshape.426
  472.8 4.5 reshape.427
  477.4 2.6 maximum_convert_fusion.6
  481.3 1.4 subtract_convert_fusion.2
  488.5 1.2 dynamic-slice_bitcast_fusion.2
  490.2 39.0 %while.18 = (s32[]{:T(128)}, bf16[8,16384]{1,0:T(8,128)(2,1)S(1)}, s32[32,2]{0,1:T(2,128)S(1)}, bf16[32,8,3168]{2,1,0:T(8,128)(2,1)S(1)}, s32[]{:T(128)}) while((s32[]{:T(128)}, bf16[8,16384]{1,0:T(8,128)(2,1)S(1)}, s32[32,2]{0,1:T(2,128)S(1)}, bf16[32,8,3168]{2,1,0:T(8,128)(2,1)S(1)}, s32[]{:T(128)}) %tuple.94), condition=%wide.while_cond, body=%wide.while_body.sunk | while | flops 2 | bytes 102497 | solution.py:56
  529.3 2.4 fusion.59
  531.7 3.6 reshape.426
  535.3 4.5 reshape.427
  539.8 2.6 maximum_convert_fusion.6
  543.8 1.4 subtract_convert_fusion.2
  546.3 1.0 copy-done.1
  547.3 627.9 %all-reduce.5.cloned.1.call-done = f32[32,32,256]{2,1,0:T(8,128)} async-done(((f32[32,32,256]{2,1,0:T(8,128)}), f32[32,32,256]{2,1,0:T(8,128)}) %all-reduce.5.cloned.1.call-update) | async-done | bytes 1048592 | tf_op jit(solution)/shard_map/psum | solution.py:183
  1175.2 1.3 fusion.50
  1176.8 3.5 collective-permute-start
  1180.3 2.4 collective-permute-start.1
  1183.0 3.9 collective-permute-done.1
  1188.8 0.9 fusion.29
  1189.7 5.1 collective-permute-start.2
  1194.9 2.1 collective-permute-start.3
  1197.0 3.7 collective-permute-done.3
  (853 shorter events, 300.5 us)
Async XLA Ops:
  6.5 0.8 copy-start
  6.5 102.5 %copy-start.3 = (s32[32]{0:T(128)S(1)}, s32[32]{0:T(128)}, u32[]{:S(2)}) copy-start(s32[32]{0:T(128)} %param.12) | copy-start | bytes 388
  6.5 102.5 %copy-start.2 = (f32[32]{0:T(128)S(1)}, f32[32]{0:T(128)}, u32[]{:S(2)}) copy-start(f32[32]{0:T(128)} %param.13) | copy-start | bytes 388
  6.5 102.4 %all-gather.4.cloned.1.call-start = ((), (), s32[]{:S(2)}) async-start(), calls=%async_computation | async-start | bytes 8650752 | tf_op jit(solution)/shard_map/all_gather | solution.py:161
  7.3 1167.9 %all-reduce.5.cloned.1.call-start = ((), (), s32[]{:S(2)}) async-start(), calls=%async_computation.1 | async-start | bytes 2097152 | tf_op jit(solution)/shard_map/psum | solution.py:183
  546.3 1.0 copy-start.1
  1176.8 6.1 collective-permute-start
  1180.3 6.6 collective-permute-start.1
  1189.7 7.3 collective-permute-start.2
  1194.9 5.8 collective-permute-start.3
Sparse Core Ops, SparseCore 0:
  9.9 98.9 all-gather.3
  547.4 627.7 all-reduce.4
where the time goes:
time: 1220 us; the launch traced here: 1210 us
  waiting for transfers between devices  657 us (54%)
  local copies, waits for them, and re-layouts  356 us (29%)
  blocking collectives  77.7 us (6%)
  other arithmetic  54.3 us (4%)
  loops' own time  33.9 us (3%)
  between operations  14.2 us (1%)
  starting transfers between devices  13.1 us (1%)
    psum x1, waiting for transfers between devices, body(): whole = lax.psum(partial_image, 'pulse')  628 us
    gather x672, local copies, waits for them, and re-layouts  269 us
    all_gather x1, blocking collectives, body(): piece_shift = lax.all_gather(pulse_shift, 'tile', axis=0, tiled=True)  40.3 us
    all_gather x1, blocking collectives, body(): piece_slope = lax.all_gather(pulse_slope, 'tile', axis=0, tiled=True)  37.3 us
    reshape x7, local copies, waits for them, and re-layouts, block_image(): segments[..., :96 * col_blocks]  31.8 us
    another operation x1, loops' own time, add_used(): return lax.fori_loop(0, (used_count + 1) // 2, add_pair, running)  29.9 us
    reshape x7, local copies, waits for them, and re-layouts, block_image(): segments[..., 96:].reshape(row_count, pulses * 2, col_blocks, 96)[..., :32]  25.1 us
  transfers between devices with their start and end apart: 6, of which 4 were waited for; matrix products, arithmetic and copies ran while one was open for 0% of the time, Pallas kernels for 0%

commit v1 on v0

--- a/solution.py
+++ b/solution.py
@@ -9,6 +9,15 @@
 step_size = 0.5
 tv_weight = 0.4
 floor_square = 0.25
+
+
+def sum_by_hops(x, name):
+    count = lax.axis_size(name)
+    total, far = (x, 1)
+    while far < count:
+        total = total + lax.ppermute(total, name, [(i, i ^ far) for i in range(count)])
+        far = 2 * far
+    return total
 
 
 def padded_2(value, sides, width):
@@ -180,7 +189,7 @@
     normalize = float(PB * tile_count * groups) ** (-0.5)
     grid_rows = tile_count * row_count
     row_anchor = tile_index * row_count
-    whole = lax.psum(partial_image, "pulse")
+    whole = sum_by_hops(partial_image, "pulse")
     base_image = to_image(whole) * normalize
     field = base_image
     for iteration in range(ITERS):

time: 1220 us -> 1300 us (1.066)
  starting transfers between devices: 13.1 us -> 151 us
  waiting for transfers between devices: 657 us -> 557 us
  local copies, waits for them, and re-layouts: 356 us -> 391 us
    psum x1 -> x0, waiting for transfers between devices: 628 us -> none  [body(): whole = lax.psum(partial_image, 'pulse')]
    ppermute x2, waiting for transfers between devices: 7.6 us -> 483 us  [padded_2(): after = lax.ppermute(leading, axis, down)]
    ppermute x0 -> x3, starting transfers between devices: none -> 138 us  [sum_by_hops(): lax.ppermute(total, name, [(i, i ^ far) for i in range(count)])]
    ppermute x0 -> x3, waiting for transfers between devices: none -> 52.2 us  [sum_by_hops(): lax.ppermute(total, name, [(i, i ^ far) for i in range(count)])]
    gather x672, local copies, waits for them, and re-layouts: 269 us -> 306 us
  transfers between devices with their start and end apart: 6 -> 8, of which waited for: 4 -> 6; matrix products, arithmetic and copies ran while one was open for 0% -> 0% of each run, Pallas kernels for 0% -> 0%
where the time goes in v1:
time: 1300 us; the launch traced here: 1290 us
  waiting for transfers between devices  557 us (43%)
  local copies, waits for them, and re-layouts  391 us (30%)
  starting transfers between devices  151 us (12%)
  blocking collectives  77.6 us (6%)
  other arithmetic  55 us (4%)
  loops' own time  36.9 us (3%)
  between operations  14.3 us (1%)
    ppermute x2, waiting for transfers between devices, padded_2(): after = lax.ppermute(leading, axis, down)  483 us
    gather x672, local copies, waits for them, and re-layouts  306 us
    ppermute x3, starting transfers between devices, sum_by_hops(): lax.ppermute(total, name, [(i, i ^ far) for i in range(count)])  138 us
    ppermute x3, waiting for transfers between devices, sum_by_hops(): lax.ppermute(total, name, [(i, i ^ far) for i in range(count)])  52.2 us
    all_gather x1, blocking collectives, body(): piece_shift = lax.all_gather(pulse_shift, 'tile', axis=0, tiled=True)  40.3 us
    all_gather x1, blocking collectives, body(): piece_slope = lax.all_gather(pulse_slope, 'tile', axis=0, tiled=True)  37.3 us
    another operation x1, loops' own time, add_used(): return lax.fori_loop(0, (used_count + 1) // 2, add_pair, running)  32.9 us
    reshape x7, local copies, waits for them, and re-layouts, block_image(): segments[..., :96 * col_blocks]  31.8 us
  transfers between devices with their start and end apart: 8, of which 6 were waited for; matrix products, arithmetic and copies ran while one was open for 0% of the time, Pallas kernels for 0%

profile of v1, /device:TPU:64, one launch (start us, length us, event | category | flops | bytes accessed | tf_op | source)
XLA Modules:
  0.0 1288.2 jit_solution(17654226696622599456)
XLA Ops:
  8.7 2.1 sort.17
  10.8 40.3 %all-gather = bf16[32,2,2]{2,1,0:T(2,128)(2,1)S(1)} all-gather(bf16[1,2,2]{2,1,0:T(2,128)(2,1)} %bitcast.74), channel_id=1, replica_groups=mesh['pulse'=8,'tile'=32] {'tile'}, dimensions={0}, use_global_device_ids=true | all-gather | bytes 264 | tf_op jit(solution)/shard_map/all_gather | solution.py:172
  51.1 37.3 %all-gather.1 = bf16[32,2,2]{2,1,0:T(2,128)(2,1)S(1)} all-gather(bf16[1,2,2]{2,1,0:T(2,128)(2,1)} %bitcast.75), channel_id=1, replica_groups=mesh['pulse'=8,'tile'=32] {'tile'}, dimensions={0}, use_global_device_ids=true | all-gather | bytes 264 | tf_op jit(solution)/shard_map/all_gather | solution.py:171
  88.5 20.5 %all-gather.4.cloned.1.call-done = bf16[64,2,2,16384]{3,2,1,0:T(2,128)(2,1)} async-done(((bf16[2,2,2,16384]{3,2,1,0:T(2,128)(2,1)}), bf16[64,2,2,16384]{3,2,1,0:T(2,128)(2,1)}) %all-gather.4.cloned.1.call-update) | async-done | bytes 8388624 | tf_op jit(solution)/shard_map/all_gather | solution.py:170
  109.1 477.6 %while.17 = (s32[]{:T(128)}, f32[32,32,256]{2,1,0:T(8,128)S(1)}, s32[]{:T(128)}, s32[64]{0:T(128)S(1)}, bf16[64,2,2,16384]{3,2,1,0:T(2,128)(2,1)}, /*index=5*/s3...) while((s32[]{:T(128)}, f32[32,32,256]{2,1,0:T(8,128)S(1)}, ...), condition=%wide.region_4.5_spmd.clone.clone, body=%wide.region_3.4_spmd.clone.clone.sunk | while | flops 548656192 | bytes 41472712 | solution.py:121
  114.3 1.2 dynamic-slice_bitcast_fusion.2
  116.0 44.3 %while.18 = (s32[]{:T(128)}, bf16[8,16384]{1,0:T(8,128)(2,1)S(1)}, s32[32,2]{0,1:T(2,128)S(1)}, bf16[32,8,3168]{2,1,0:T(8,128)(2,1)S(1)}, s32[]{:T(128)}) while((s32[]{:T(128)}, bf16[8,16384]{1,0:T(8,128)(2,1)S(1)}, s32[32,2]{0,1:T(2,128)S(1)}, bf16[32,8,3168]{2,1,0:T(8,128)(2,1)S(1)}, s32[]{:T(128)}) %tuple.94), condition=%wide.while_cond, body=%wide.while_body.sunk | while | flops 2 | bytes 102497 | solution.py:65
  160.3 2.4 fusion.59
  162.8 3.6 reshape.426
  166.4 4.5 reshape.427
  170.9 2.6 maximum_convert_fusion.6
  174.8 1.4 subtract_convert_fusion.2
  182.5 1.2 dynamic-slice_bitcast_fusion.2
  184.2 44.3 %while.18 = (s32[]{:T(128)}, bf16[8,16384]{1,0:T(8,128)(2,1)S(1)}, s32[32,2]{0,1:T(2,128)S(1)}, bf16[32,8,3168]{2,1,0:T(8,128)(2,1)S(1)}, s32[]{:T(128)}) while((s32[]{:T(128)}, bf16[8,16384]{1,0:T(8,128)(2,1)S(1)}, s32[32,2]{0,1:T(2,128)S(1)}, bf16[32,8,3168]{2,1,0:T(8,128)(2,1)S(1)}, s32[]{:T(128)}) %tuple.94), condition=%wide.while_cond, body=%wide.while_body.sunk | while | flops 2 | bytes 102497 | solution.py:65
  228.5 2.4 fusion.59
  231.0 3.6 reshape.426
  234.6 4.5 reshape.427
  239.1 2.6 maximum_convert_fusion.6
  243.0 1.4 subtract_convert_fusion.2
  250.7 1.2 dynamic-slice_bitcast_fusion.2
  252.4 44.3 %while.18 = (s32[]{:T(128)}, bf16[8,16384]{1,0:T(8,128)(2,1)S(1)}, s32[32,2]{0,1:T(2,128)S(1)}, bf16[32,8,3168]{2,1,0:T(8,128)(2,1)S(1)}, s32[]{:T(128)}) while((s32[]{:T(128)}, bf16[8,16384]{1,0:T(8,128)(2,1)S(1)}, s32[32,2]{0,1:T(2,128)S(1)}, bf16[32,8,3168]{2,1,0:T(8,128)(2,1)S(1)}, s32[]{:T(128)}) %tuple.94), condition=%wide.while_cond, body=%wide.while_body.sunk | while | flops 2 | bytes 102497 | solution.py:65
  296.8 2.4 fusion.59
  299.2 3.6 reshape.426
  302.8 4.5 reshape.427
  307.3 2.6 maximum_convert_fusion.6
  311.3 1.4 subtract_convert_fusion.2
  319.0 1.2 dynamic-slice_bitcast_fusion.2
  320.6 44.3 %while.18 = (s32[]{:T(128)}, bf16[8,16384]{1,0:T(8,128)(2,1)S(1)}, s32[32,2]{0,1:T(2,128)S(1)}, bf16[32,8,3168]{2,1,0:T(8,128)(2,1)S(1)}, s32[]{:T(128)}) while((s32[]{:T(128)}, bf16[8,16384]{1,0:T(8,128)(2,1)S(1)}, s32[32,2]{0,1:T(2,128)S(1)}, bf16[32,8,3168]{2,1,0:T(8,128)(2,1)S(1)}, s32[]{:T(128)}) %tuple.94), condition=%wide.while_cond, body=%wide.while_body.sunk | while | flops 2 | bytes 102497 | solution.py:65
  365.0 2.4 fusion.59
  367.4 3.6 reshape.426
  371.0 4.5 reshape.427
  375.6 2.6 maximum_convert_fusion.6
  379.5 1.4 subtract_convert_fusion.2
  387.2 1.2 dynamic-slice_bitcast_fusion.2
  388.9 44.3 %while.18 = (s32[]{:T(128)}, bf16[8,16384]{1,0:T(8,128)(2,1)S(1)}, s32[32,2]{0,1:T(2,128)S(1)}, bf16[32,8,3168]{2,1,0:T(8,128)(2,1)S(1)}, s32[]{:T(128)}) while((s32[]{:T(128)}, bf16[8,16384]{1,0:T(8,128)(2,1)S(1)}, s32[32,2]{0,1:T(2,128)S(1)}, bf16[32,8,3168]{2,1,0:T(8,128)(2,1)S(1)}, s32[]{:T(128)}) %tuple.94), condition=%wide.while_cond, body=%wide.while_body.sunk | while | flops 2 | bytes 102497 | solution.py:65
  433.2 2.4 fusion.59
  435.7 3.6 reshape.426
  439.3 4.5 reshape.427
  443.8 2.6 maximum_convert_fusion.6
  447.7 1.4 subtract_convert_fusion.2
  455.4 1.2 dynamic-slice_bitcast_fusion.2
  457.1 44.3 %while.18 = (s32[]{:T(128)}, bf16[8,16384]{1,0:T(8,128)(2,1)S(1)}, s32[32,2]{0,1:T(2,128)S(1)}, bf16[32,8,3168]{2,1,0:T(8,128)(2,1)S(1)}, s32[]{:T(128)}) while((s32[]{:T(128)}, bf16[8,16384]{1,0:T(8,128)(2,1)S(1)}, s32[32,2]{0,1:T(2,128)S(1)}, bf16[32,8,3168]{2,1,0:T(8,128)(2,1)S(1)}, s32[]{:T(128)}) %tuple.94), condition=%wide.while_cond, body=%wide.while_body.sunk | while | flops 2 | bytes 102497 | solution.py:65
  501.4 2.4 fusion.59
  503.9 3.6 reshape.426
  507.5 4.5 reshape.427
  512.0 2.6 maximum_convert_fusion.6
  515.9 1.4 subtract_convert_fusion.2
  523.6 1.2 dynamic-slice_bitcast_fusion.2
  525.3 44.3 %while.18 = (s32[]{:T(128)}, bf16[8,16384]{1,0:T(8,128)(2,1)S(1)}, s32[32,2]{0,1:T(2,128)S(1)}, bf16[32,8,3168]{2,1,0:T(8,128)(2,1)S(1)}, s32[]{:T(128)}) while((s32[]{:T(128)}, bf16[8,16384]{1,0:T(8,128)(2,1)S(1)}, s32[32,2]{0,1:T(2,128)S(1)}, bf16[32,8,3168]{2,1,0:T(8,128)(2,1)S(1)}, s32[]{:T(128)}) %tuple.94), condition=%wide.while_cond, body=%wide.while_body.sunk | while | flops 2 | bytes 102497 | solution.py:65
  569.7 2.4 fusion.59
  572.1 3.6 reshape.426
  575.7 4.5 reshape.427
  580.3 2.6 maximum_convert_fusion.6
  584.2 1.4 subtract_convert_fusion.2
  586.8 2.6 collective-permute-done
  589.6 138.0 %collective-permute-start.1 = (f32[32,32,256]{2,1,0:T(8,128)S(1)}, f32[32,32,256]{2,1,0:T(8,128)S(1)}, u32[]{:S(2)}, u32[]{:S(2)}) collective-permute-start(f32[32,32,256]{2,1,0:T(8,128)S(1)} %add.309), channel_id=1, source_target_pairs={{0,64},{32,96},{64,0},{96,32},{128,192},{160,224},{192,128},{224,1... | collective-permute-start | bytes 3145736 | tf_op jit(solution)/shard_map/ppermute | solution.py:18
  727.6 23.5 %collective-permute-done.1 = f32[32,32,256]{2,1,0:T(8,128)S(1)} collective-permute-done((f32[32,32,256]{2,1,0:T(8,128)S(1)}, f32[32,32,256]{2,1,0:T(8,128)S(1)}, u32[]{:S(2)}, u32[]{:S(2)}) %collective-permute-start.1) | collective-permute-done | bytes 1048608 | tf_op jit(solution)/shard_map/ppermute | solution.py:18
  751.4 26.1 %collective-permute-done.2 = f32[32,32,256]{2,1,0:T(8,128)S(1)} collective-permute-done((f32[32,32,256]{2,1,0:T(8,128)S(1)}, f32[32,32,256]{2,1,0:T(8,128)S(1)}, u32[]{:S(2)}, u32[]{:S(2)}) %collective-permute-start.2) | collective-permute-done | bytes 1048608 | tf_op jit(solution)/shard_map/ppermute | solution.py:18
  778.2 3.9 collective-permute-start.3
  782.1 2.1 collective-permute-start.4
  784.5 479.5 %collective-permute-done.4 = f32[2,1,4096]{2,1,0:T(1,128)S(1)} collective-permute-done((f32[2,1,4096]{2,1,0:T(1,128)S(1)}, f32[2,1,4096]{2,1,0:T(1,128)S(1)}, u32[]{:S(2)}, u32[]{:S(2)}) %collective-permute-start.4) | collective-permute-done | bytes 32800 | tf_op jit(solution)/shard_map/ppermute | solution.py:31
  1266.8 5.1 collective-permute-start.5
  1272.0 1.9 collective-permute-start.6
  1273.9 3.9 collective-permute-done.6
  (857 shorter events, 339.7 us)
Async XLA Ops:
  6.5 0.7 copy-start
  6.5 102.5 %copy-start.2 = (s32[32]{0:T(128)S(1)}, s32[32]{0:T(128)}, u32[]{:S(2)}) copy-start(s32[32]{0:T(128)} %param.12) | copy-start | bytes 388
  6.5 102.5 %copy-start.1 = (f32[32]{0:T(128)S(1)}, f32[32]{0:T(128)}, u32[]{:S(2)}) copy-start(f32[32]{0:T(128)} %param.13) | copy-start | bytes 388
  6.5 102.4 %all-gather.4.cloned.1.call-start = ((), (), s32[]{:S(2)}) async-start(), calls=%async_computation | async-start | bytes 8650752 | tf_op jit(solution)/shard_map/all_gather | solution.py:170
  586.7 2.7 collective-permute-start
  589.6 161.5 %collective-permute-start.1 = (f32[32,32,256]{2,1,0:T(8,128)S(1)}, f32[32,32,256]{2,1,0:T(8,128)S(1)}, u32[]{:S(2)}, u32[]{:S(2)}) collective-permute-start(f32[32,32,256]{2,1,0:T(8,128)S(1)} %add.309), channel_id=1, source_target_pairs={{0,64},{32,96},{64,0},{96,32},{128,192},{160,224},{192,128},{224,1... | collective-permute-start | bytes 3145736 | tf_op jit(solution)/shard_map/ppermute | solution.py:18
  751.3 26.2 %collective-permute-start.2 = (f32[32,32,256]{2,1,0:T(8,128)S(1)}, f32[32,32,256]{2,1,0:T(8,128)S(1)}, u32[]{:S(2)}, u32[]{:S(2)}) collective-permute-start(f32[32,32,256]{2,1,0:T(8,128)S(1)} %add.310), channel_id=1, source_target_pairs={{0,128},{32,160},{64,192},{96,224},{128,0},{160,32},{192,64},{224,... | collective-permute-start | bytes 3145736 | tf_op jit(solution)/shard_map/ppermute | solution.py:18
  778.2 6.3 collective-permute-start.3
  782.1 481.8 %collective-permute-start.4 = (f32[2,1,4096]{2,1,0:T(1,128)S(1)}, f32[2,1,4096]{2,1,0:T(1,128)S(1)}, u32[]{:S(2)}, u32[]{:S(2)}) collective-permute-start(f32[2,1,4096]{2,1,0:T(1,128)S(1)} %get-tuple-element.323), channel_id=1, source_target_pairs={{1,0},{2,1},{3,2},{4,3},{5,4},{6,5},{7,6},{8,7},{9,8},{10,9},{11,1... | collective-permute-start | bytes 98312 | tf_op jit(solution)/shard_map/ppermute | solution.py:31
  1266.8 7.1 collective-permute-start.5
  1272.0 5.8 collective-permute-start.6
Sparse Core Ops, SparseCore 0:
  9.9 98.9 all-gather.3
